TPU v7x, 256 devices: a whole 4x4x8 slice. The times are simulated.
256 devices in a mesh: phase: 64 (over y, z, core), sect: 4 (over x).
Axes of the slice: x: 4, y: 4, z: 8, core: 2. Of those that a mesh axis runs over, the one named last changes fastest.
Arguments:
- activations: bfloat16 [8192, 32768], P('phase', 'sect'), may hold values from 0 to 2
- block_tiles: bfloat16 [64, 512, 8, 4096], P('phase', 'sect'), may hold values from -0.25 to 0.25
- sources: int32 [64, 512, 8], P('phase', 'sect'), may hold values from 0 to 511, all different within a row
- layer_bias: float32 [64], P('phase'), may hold values from -0.6 to -0.2
Outputs:
- next_acts: bfloat16 [8192, 32768], P('phase', 'sect')
Inputs may be any that keep to these rules, and one draw needn't show every extreme that they name: `sources`: each row of 8 entries names distinct input blocks.
All inputs are finite; a program needn't handle non-finite values.
Results may differ from a plain program's by a relative error of at most 0.0055.
Values may be sent and summed in bfloat16 or wider, within the bound.
A program may use at most 128 MiB of HBM per device.

v0:
```python
import functools

import jax
import jax.numpy as jnp
from jax import lax
from jax.experimental import pallas as pl
from jax.experimental.pallas import tpu as pltpu
from jax.sharding import PartitionSpec as P

BLK = 64
CHUNKS = 4
JB = 8


def from_behind(array, axis, by):
    size = lax.axis_size(axis)
    return lax.ppermute(array, axis, [(i, (i + by) % size) for i in range(size)])


def product_kernel(fanin, src_ref, x_ref, w_ref, b_ref, o_ref):
    g = pl.program_id(0)
    bias = b_ref[0]
    rows = x_ref.shape[0]
    lane = lax.broadcasted_iota(jnp.int32, (rows, 2 * BLK), 1)
    outs = []
    for jj in range(JB):
        j = g * JB + jj
        pairs = []
        for m in range(fanin // 2):
            halves = []
            for h in range(2):
                s = src_ref[j * fanin + 2 * m + h]
                start = pl.multiple_of((s // 2) * (2 * BLK), 2 * BLK)
                x = x_ref[:, pl.ds(start, 2 * BLK)]
                swapped = pltpu.roll(x, BLK, 1)
                keep = (s % 2) == h
                halves.append(jnp.where(keep, x, swapped))
            pairs.append(jnp.where(lane < BLK, halves[0], halves[1]))
        a = jnp.concatenate(pairs, axis=1)
        acc = jnp.dot(a, w_ref[jj], preferred_element_type=jnp.float32)
        outs.append(jnp.maximum(acc + bias, 0.0).astype(o_ref.dtype))
    o_ref[...] = jnp.concatenate(outs, axis=1)


def block_layer(gathered, weights, src_flat, layer_bias):
    rows, width = gathered.shape
    nblk, depth, _ = weights.shape
    fanin = depth // BLK
    return pl.pallas_call(
        functools.partial(product_kernel, fanin),
        grid_spec=pltpu.PrefetchScalarGridSpec(
            num_scalar_prefetch=1,
            grid=(nblk // JB,),
            in_specs=[
                pl.BlockSpec((rows, width), lambda g, s: (0, 0)),
                pl.BlockSpec((JB, depth, BLK), lambda g, s: (g, 0, 0)),
                pl.BlockSpec(memory_space=pltpu.SMEM),
            ],
            out_specs=pl.BlockSpec((rows, JB * BLK), lambda g, s: (0, g)),
        ),
        out_shape=jax.ShapeDtypeStruct((rows, nblk * BLK), jnp.bfloat16),
        compiler_params=pltpu.CompilerParams(vmem_limit_bytes=48 * 1024 * 1024),
    )(src_flat, gathered, weights, layer_bias)


def layer(quarter, weights, src_flat, layer_bias):
    gathered = lax.all_gather(quarter, "sect", axis=1, tiled=True)
    return block_layer(gathered, weights, src_flat, layer_bias)


def per_device(activations, block_tiles, sources, layer_bias):
    nblk, fanin = sources.shape[1], sources.shape[2]
    weights = block_tiles[0].reshape(nblk, fanin * BLK, BLK)
    src_flat = sources[0].reshape(-1)
    rows = activations.shape[0] // CHUNKS
    outs = []
    for c in range(CHUNKS):
        part = activations[c * rows:(c + 1) * rows]
        hidden = layer(part, weights, src_flat, layer_bias)
        moved = from_behind(hidden, "phase", 1)
        hidden = layer(moved, weights, src_flat, layer_bias)
        outs.append(from_behind(hidden, "phase", 1))
    return jnp.concatenate(outs, axis=0)


def solution(mesh):
    in_specs = (
        P("phase", "sect"),
        P("phase", "sect", None, None),
        P("phase", "sect", None),
        P("phase"),
    )
    out_specs = P("phase", "sect")
    return jax.shard_map(
        per_device, mesh=mesh, in_specs=in_specs, out_specs=out_specs, check_vma=False
    )
```

profile of v0, /device:TPU:6, one launch (start us, length us, event | category | flops | bytes accessed | tf_op | source)
XLA Modules:
  0.0 330.1 jit_solution(1588821038386893776)
XLA Ops:
  6.5 2.9 fusion
  9.5 0.7 all-gather.13.cloned.1.call-update
  10.3 0.7 all-gather.17.cloned.1.call-update
  11.0 0.5 all-gather.21.cloned.1.call-update
  11.6 12.5 %copy.6 = bf16[1,128,8,4096]{1,3,2,0:T(8,128)(2,1)} copy(bf16[1,128,8,4096]{3,2,1,0:T(8,128)(2,1)} %param.5) | data formatting | bytes 16777216 | tf_op args[1]
  24.1 23.9 %copy.7.w_ref = bf16[128,512,64]{2,1,0:T(8,128)(2,1)} copy(bf16[128,512,64]{0,2,1:T(8,128)(2,1)} %bitcast.1) | data formatting | bytes 16777216 | tf_op jit(solution)/shard_map/reshape;squeeze | solution.py:73
  48.0 0.1 copy.5
  48.1 0.1 reshape_squeeze.6.src_ref
  48.8 1.6 copy-done.6
  50.4 17.7 %shard_map.46 = bf16[32,8192]{1,0:T(8,128)(2,1)S(1)} custom-call(s32[1024]{0:T(1024)S(1)} %reshape_squeeze.6.src_ref, bf16[32,32768]{1,0:T(8,128)(2,1)S(1)} %copy-done.6, bf16[128,512,64]{2,1,0:T(8,128)(2,1)} %copy.7.w_ref, f32[1]{0:T(128)S(6)} %copy.15.b_ref), custom_call_target="tpu_custom_call" | custom-call | tf_op jit(solution)/shard_map/pallas_call | solution.py:49
  68.1 0.1 collective-permute-start
  68.2 14.6 %collective-permute-done = bf16[32,8192]{1,0:T(8,128)(2,1)S(1)} collective-permute-done((bf16[32,8192]{1,0:T(8,128)(2,1)S(1)}, bf16[32,8192]{1,0:T(8,128)(2,1)S(1)}, u32[]{:S(2)}, u32[]{:S(2)}) %collective-permute-start) | collective-permute-done | bytes 524320 | tf_op jit(solution)/shard_map/ppermute | solution.py:17
  82.8 0.8 copy-done.8
  83.7 1.6 copy-done.4
  85.3 17.7 %shard_map.48 = bf16[32,8192]{1,0:T(8,128)(2,1)S(1)} custom-call(s32[1024]{0:T(1024)S(1)} %reshape_squeeze.6.src_ref, bf16[32,32768]{1,0:T(8,128)(2,1)S(1)} %copy-done.4, bf16[128,512,64]{2,1,0:T(8,128)(2,1)} %copy.7.w_ref, f32[1]{0:T(128)S(6)} %copy.15.b_ref), custom_call_target="tpu_custom_call" | custom-call | tf_op jit(solution)/shard_map/pallas_call | solution.py:49
  103.1 0.1 collective-permute-start.2
  103.1 11.9 %collective-permute-done.2 = bf16[32,8192]{1,0:T(8,128)(2,1)S(1)} collective-permute-done((bf16[32,8192]{1,0:T(8,128)(2,1)S(1)}, bf16[32,8192]{1,0:T(8,128)(2,1)S(1)}, u32[]{:S(2)}, u32[]{:S(2)}) %collective-permute-start.2) | collective-permute-done | bytes 524320 | tf_op jit(solution)/shard_map/ppermute | solution.py:17
  115.0 0.8 copy-done.9
  116.0 1.6 copy-done.2
  117.6 17.8 %shard_map.50 = bf16[32,8192]{1,0:T(8,128)(2,1)S(1)} custom-call(s32[1024]{0:T(1024)S(1)} %reshape_squeeze.6.src_ref, bf16[32,32768]{1,0:T(8,128)(2,1)S(1)} %copy-done.2, bf16[128,512,64]{2,1,0:T(8,128)(2,1)} %copy.7.w_ref, f32[1]{0:T(128)S(6)} %copy.15.b_ref), custom_call_target="tpu_custom_call" | custom-call | tf_op jit(solution)/shard_map/pallas_call | solution.py:49
  135.3 0.1 collective-permute-start.4
  135.4 11.9 %collective-permute-done.4 = bf16[32,8192]{1,0:T(8,128)(2,1)S(1)} collective-permute-done((bf16[32,8192]{1,0:T(8,128)(2,1)S(1)}, bf16[32,8192]{1,0:T(8,128)(2,1)S(1)}, u32[]{:S(2)}, u32[]{:S(2)}) %collective-permute-start.4) | collective-permute-done | bytes 524320 | tf_op jit(solution)/shard_map/ppermute | solution.py:17
  147.3 0.8 copy-done.10
  148.1 0.0 all-gather.23.cloned.1.call-start
  148.2 1.5 all-gather.21.cloned.1.call-done.x_ref
  149.7 1.6 copy-done
  151.3 17.7 %shard_map.52 = bf16[32,8192]{1,0:T(8,128)(2,1)S(1)} custom-call(s32[1024]{0:T(1024)S(1)} %reshape_squeeze.6.src_ref, bf16[32,32768]{1,0:T(8,128)(2,1)S(1)} %copy-done, bf16[128,512,64]{2,1,0:T(8,128)(2,1)} %copy.7.w_ref, f32[1]{0:T(128)S(6)} %copy.15.b_ref), custom_call_target="tpu_custom_call" | custom-call | tf_op jit(solution)/shard_map/pallas_call | solution.py:49
  169.0 0.1 collective-permute-start.6
  169.1 11.9 %collective-permute-done.6 = bf16[32,8192]{1,0:T(8,128)(2,1)S(1)} collective-permute-done((bf16[32,8192]{1,0:T(8,128)(2,1)S(1)}, bf16[32,8192]{1,0:T(8,128)(2,1)S(1)}, u32[]{:S(2)}, u32[]{:S(2)}) %collective-permute-start.6) | collective-permute-done | bytes 524320 | tf_op jit(solution)/shard_map/ppermute | solution.py:17
  181.0 0.8 copy-done.11
  181.8 3.1 all-gather.11.cloned.1.call-done.x_ref
  184.9 1.6 copy-done.1
  186.5 17.7 %shard_map.47 = bf16[32,8192]{1,0:T(8,128)(2,1)S(1)} custom-call(s32[1024]{0:T(1024)S(1)} %reshape_squeeze.6.src_ref, bf16[32,32768]{1,0:T(8,128)(2,1)S(1)} %copy-done.1, bf16[128,512,64]{2,1,0:T(8,128)(2,1)} %copy.7.w_ref, f32[1]{0:T(128)S(6)} %copy.15.b_ref), custom_call_target="tpu_custom_call" | custom-call | tf_op jit(solution)/shard_map/pallas_call | solution.py:49
  204.2 0.1 collective-permute-start.1
  204.2 15.8 %all-gather.15.cloned.1.call-done.x_ref = bf16[32,32768]{1,0:T(8,128)(2,1)} async-done(((bf16[32,8192]{1,0:T(8,128)(2,1)}), bf16[32,32768]{1,0:T(8,128)(2,1)}) %all-gather.15.cloned.1.call-update) | async-done | bytes 2097168 | tf_op jit(solution)/shard_map/all_gather | solution.py:67
  220.0 1.6 copy-done.3
  221.6 17.7 %shard_map.49 = bf16[32,8192]{1,0:T(8,128)(2,1)S(1)} custom-call(s32[1024]{0:T(1024)S(1)} %reshape_squeeze.6.src_ref, bf16[32,32768]{1,0:T(8,128)(2,1)S(1)} %copy-done.3, bf16[128,512,64]{2,1,0:T(8,128)(2,1)} %copy.7.w_ref, f32[1]{0:T(128)S(6)} %copy.15.b_ref), custom_call_target="tpu_custom_call" | custom-call | tf_op jit(solution)/shard_map/pallas_call | solution.py:49
  239.3 0.2 collective-permute-start.3
  239.5 15.8 %all-gather.19.cloned.1.call-done.x_ref = bf16[32,32768]{1,0:T(8,128)(2,1)} async-done(((bf16[32,8192]{1,0:T(8,128)(2,1)}), bf16[32,32768]{1,0:T(8,128)(2,1)}) %all-gather.19.cloned.1.call-update) | async-done | bytes 2097168 | tf_op jit(solution)/shard_map/all_gather | solution.py:67
  255.3 1.6 copy-done.5
  256.9 17.7 %shard_map.51 = bf16[32,8192]{1,0:T(8,128)(2,1)S(1)} custom-call(s32[1024]{0:T(1024)S(1)} %reshape_squeeze.6.src_ref, bf16[32,32768]{1,0:T(8,128)(2,1)S(1)} %copy-done.5, bf16[128,512,64]{2,1,0:T(8,128)(2,1)} %copy.7.w_ref, f32[1]{0:T(128)S(6)} %copy.15.b_ref), custom_call_target="tpu_custom_call" | custom-call | tf_op jit(solution)/shard_map/pallas_call | solution.py:49
  274.6 0.1 collective-permute-start.5
  274.7 15.9 %all-gather.23.cloned.1.call-done.x_ref = bf16[32,32768]{1,0:T(8,128)(2,1)} async-done(((bf16[32,8192]{1,0:T(8,128)(2,1)}), bf16[32,32768]{1,0:T(8,128)(2,1)}) %all-gather.23.cloned.1.call-update) | async-done | bytes 2097168 | tf_op jit(solution)/shard_map/all_gather | solution.py:67
  290.6 1.6 copy-done.7
  292.2 17.6 %shard_map.53 = bf16[32,8192]{1,0:T(8,128)(2,1)S(1)} custom-call(s32[1024]{0:T(1024)S(1)} %reshape_squeeze.6.src_ref, bf16[32,32768]{1,0:T(8,128)(2,1)S(1)} %copy-done.7, bf16[128,512,64]{2,1,0:T(8,128)(2,1)} %copy.7.w_ref, f32[1]{0:T(128)S(6)} %copy.15.b_ref), custom_call_target="tpu_custom_call" | custom-call | tf_op jit(solution)/shard_map/pallas_call | solution.py:49
  309.8 0.1 collective-permute-start.7
  309.9 11.9 %collective-permute-done.7 = bf16[32,8192]{1,0:T(8,128)(2,1)S(1)} collective-permute-done((bf16[32,8192]{1,0:T(8,128)(2,1)S(1)}, bf16[32,8192]{1,0:T(8,128)(2,1)S(1)}, u32[]{:S(2)}, u32[]{:S(2)}) %collective-permute-start.7) | collective-permute-done | bytes 524320 | tf_op jit(solution)/shard_map/ppermute | solution.py:17
  321.8 1.5 pad_maximum_fusion
  (32 shorter events, 0.4 us)
Async XLA Ops:
  6.5 42.3 %all-gather.9.cloned.1.call-start = ((), (), s32[]{:S(2)}) async-start(), calls=%async_computation | async-start | bytes 2621440 | tf_op jit(solution)/shard_map/all_gather | solution.py:67
  9.5 74.3 %all-gather.13.cloned.1.call-start = ((), (), s32[]{:S(2)}) async-start(), calls=%async_computation.2 | async-start | bytes 2621440 | tf_op jit(solution)/shard_map/all_gather | solution.py:67
  10.2 105.8 %all-gather.17.cloned.1.call-start = ((), (), s32[]{:S(2)}) async-start(), calls=%async_computation.4 | async-start | bytes 2621440 | tf_op jit(solution)/shard_map/all_gather | solution.py:67
  10.9 138.8 %all-gather.21.cloned.1.call-start = ((), (), s32[]{:S(2)}) async-start(), calls=%async_computation.6 | async-start | bytes 2621440 | tf_op jit(solution)/shard_map/all_gather | solution.py:67
  11.5 173.3 %all-gather.11.cloned.1.call-start = ((), (), s32[]{:S(2)}) async-start(), calls=%async_computation.1 | async-start | bytes 2621440 | tf_op jit(solution)/shard_map/all_gather | solution.py:67
  24.1 23.9 %copy-start.12 = (s32[1,128,8]{1,2,0:T(8,128)S(1)}, s32[1,128,8]{1,2,0:T(8,128)}, u32[]{:S(2)}) copy-start(s32[1,128,8]{1,2,0:T(8,128)} %param.6) | copy-start | bytes 12292
  48.8 1.6 copy-start.6
  68.1 14.7 %collective-permute-start = (bf16[32,8192]{1,0:T(8,128)(2,1)S(1)}, bf16[32,8192]{1,0:T(8,128)(2,1)S(1)}, u32[]{:S(2)}, u32[]{:S(2)}) collective-permute-start(bf16[32,8192]{1,0:T(8,128)(2,1)S(1)} %shard_map.46), channel_id=1, source_target_pairs={{0,4},{4,8},{8,12},{12,16},{16,20},{20,24},{24,28},{28,32},{32,36}... | collective-permute-start | bytes 1572872 | tf_op jit(solution)/shard_map/ppermute | solution.py:17
  82.8 0.8 copy-start.8
  83.7 136.3 %all-gather.15.cloned.1.call-start = ((), (), s32[]{:S(2)}) async-start(), calls=%async_computation.3 | async-start | bytes 2621440 | tf_op jit(solution)/shard_map/all_gather | solution.py:67
  83.7 1.6 copy-start.4
  103.1 12.0 %collective-permute-start.2 = (bf16[32,8192]{1,0:T(8,128)(2,1)S(1)}, bf16[32,8192]{1,0:T(8,128)(2,1)S(1)}, u32[]{:S(2)}, u32[]{:S(2)}) collective-permute-start(bf16[32,8192]{1,0:T(8,128)(2,1)S(1)} %shard_map.48), channel_id=1, source_target_pairs={{0,4},{4,8},{8,12},{12,16},{16,20},{20,24},{24,28},{28,32},{32,36}... | collective-permute-start | bytes 1572872 | tf_op jit(solution)/shard_map/ppermute | solution.py:17
  115.0 0.8 copy-start.9
  115.9 139.4 %all-gather.19.cloned.1.call-start = ((), (), s32[]{:S(2)}) async-start(), calls=%async_computation.5 | async-start | bytes 2621440 | tf_op jit(solution)/shard_map/all_gather | solution.py:67
  116.0 1.6 copy-start.2
  135.3 12.0 %collective-permute-start.4 = (bf16[32,8192]{1,0:T(8,128)(2,1)S(1)}, bf16[32,8192]{1,0:T(8,128)(2,1)S(1)}, u32[]{:S(2)}, u32[]{:S(2)}) collective-permute-start(bf16[32,8192]{1,0:T(8,128)(2,1)S(1)} %shard_map.50), channel_id=1, source_target_pairs={{0,4},{4,8},{8,12},{12,16},{16,20},{20,24},{24,28},{28,32},{32,36}... | collective-permute-start | bytes 1572872 | tf_op jit(solution)/shard_map/ppermute | solution.py:17
  147.3 0.8 copy-start.10
  148.1 142.4 %all-gather.23.cloned.1.call-start = ((), (), s32[]{:S(2)}) async-start(), calls=%async_computation.7 | async-start | bytes 2621440 | tf_op jit(solution)/shard_map/all_gather | solution.py:67
  149.7 1.6 copy-start
  169.0 12.0 %collective-permute-start.6 = (bf16[32,8192]{1,0:T(8,128)(2,1)S(1)}, bf16[32,8192]{1,0:T(8,128)(2,1)S(1)}, u32[]{:S(2)}, u32[]{:S(2)}) collective-permute-start(bf16[32,8192]{1,0:T(8,128)(2,1)S(1)} %shard_map.52), channel_id=1, source_target_pairs={{0,4},{4,8},{8,12},{12,16},{16,20},{20,24},{24,28},{28,32},{32,36}... | collective-permute-start | bytes 1572872 | tf_op jit(solution)/shard_map/ppermute | solution.py:17
  181.0 0.8 copy-start.11
  184.9 1.6 copy-start.1
  204.2 105.7 %collective-permute-start.1 = (bf16[32,8192]{1,0:T(8,128)(2,1)S(1)}, bf16[32,8192]{1,0:T(8,128)(2,1)S(1)}, u32[]{:S(2)}, u32[]{:S(2)}) collective-permute-start(bf16[32,8192]{1,0:T(8,128)(2,1)S(1)} %shard_map.47), channel_id=1, source_target_pairs={{0,4},{4,8},{8,12},{12,16},{16,20},{20,24},{24,28},{28,32},{32,36}... | collective-permute-start | bytes 1572872 | tf_op jit(solution)/shard_map/ppermute | solution.py:17
  220.0 1.6 copy-start.3
  239.3 70.6 %collective-permute-start.3 = (bf16[32,8192]{1,0:T(8,128)(2,1)S(1)}, bf16[32,8192]{1,0:T(8,128)(2,1)S(1)}, u32[]{:S(2)}, u32[]{:S(2)}) collective-permute-start(bf16[32,8192]{1,0:T(8,128)(2,1)S(1)} %shard_map.49), channel_id=1, source_target_pairs={{0,4},{4,8},{8,12},{12,16},{16,20},{20,24},{24,28},{28,32},{32,36}... | collective-permute-start | bytes 1572872 | tf_op jit(solution)/shard_map/ppermute | solution.py:17
  255.3 1.6 copy-start.5
  274.6 35.3 %collective-permute-start.5 = (bf16[32,8192]{1,0:T(8,128)(2,1)S(1)}, bf16[32,8192]{1,0:T(8,128)(2,1)S(1)}, u32[]{:S(2)}, u32[]{:S(2)}) collective-permute-start(bf16[32,8192]{1,0:T(8,128)(2,1)S(1)} %shard_map.51), channel_id=1, source_target_pairs={{0,4},{4,8},{8,12},{12,16},{16,20},{20,24},{24,28},{28,32},{32,36}... | collective-permute-start | bytes 1572872 | tf_op jit(solution)/shard_map/ppermute | solution.py:17
  290.6 1.6 copy-start.7
  309.8 12.0 %collective-permute-start.7 = (bf16[32,8192]{1,0:T(8,128)(2,1)S(1)}, bf16[32,8192]{1,0:T(8,128)(2,1)S(1)}, u32[]{:S(2)}, u32[]{:S(2)}) collective-permute-start(bf16[32,8192]{1,0:T(8,128)(2,1)S(1)} %shard_map.53), channel_id=1, source_target_pairs={{0,4},{4,8},{8,12},{12,16},{16,20},{20,24},{24,28},{28,32},{32,36}... | collective-permute-start | bytes 1572872 | tf_op jit(solution)/shard_map/ppermute | solution.py:17
Sparse Core Ops, SparseCore 0:
  9.6 34.4 all-gather.8
  45.8 33.4 all-gather.12
  81.1 33.4 all-gather.16
  116.2 33.4 all-gather.20
  151.4 33.4 all-gather.10
  186.5 33.4 all-gather.14
  221.8 33.4 all-gather.18
  257.1 33.4 all-gather.22
where the time goes:
time: 335 us; the launch traced here: 330 us
  Pallas kernels  142 us (42%)
  waiting for transfers between devices  116 us (35%)
  local copies, waits for them, and re-layouts  55.4 us (17%)
  between operations  14.3 us (4%)
    pallas_call x8, Pallas kernels, block_layer(): pl.pallas_call(functools.partial(product_kernel, fanin), grid_spec=pltpu....  142 us
    ppermute x8, waiting for transfers between devices, from_behind(): lax.ppermute(array, axis, [(i, (i + by) % size) for i in range(size)])  62.2 us
    all_gather x8, waiting for transfers between devices, layer(): gathered = lax.all_gather(quarter, 'sect', axis=1, tiled=True)  52.1 us
    unnamed x28, local copies, waits for them, and re-layouts  28.5 us
    another operation x1, local copies, waits for them, and re-layouts, per_device(): weights = block_tiles[0].reshape(nblk, fanin * BLK, BLK)  23.9 us
  transfers between devices with their start and end apart: 16, of which 10 were waited for; matrix products, arithmetic and copies ran while one was open for 11% of the time, Pallas kernels for 43%

commit v1 on v0

--- a/solution.py
+++ b/solution.py
@@ -8,7 +8,7 @@
 from jax.sharding import PartitionSpec as P
 
 BLK = 64
-CHUNKS = 4
+CHUNKS = 2
 JB = 8
 
 
@@ -60,6 +60,11 @@
         ),
         out_shape=jax.ShapeDtypeStruct((rows, nblk * BLK), jnp.bfloat16),
         compiler_params=pltpu.CompilerParams(vmem_limit_bytes=48 * 1024 * 1024),
+        cost_estimate=pl.CostEstimate(
+            flops=2 * nblk * depth * 256 * 256,
+            bytes_accessed=2 * (weights.size + gathered.size + rows * nblk * BLK),
+            transcendentals=0,
+        ),
     )(src_flat, gathered, weights, layer_bias)
 
 

time: 335 us -> 271 us (0.81)
  Pallas kernels: 142 us -> 76.3 us
  waiting for transfers between devices: 116 us -> 125 us
  local copies, waits for them, and re-layouts: 55.4 us -> 50.5 us
    pallas_call x8 -> x4, Pallas kernels: 142 us -> 76.3 us  [block_layer(): pl.pallas_call(functools.partial(product_kernel, fanin), grid_spec=pltpu....]
    all_gather x8 -> x4, waiting for transfers between devices: 52.1 us -> 71.3 us  [layer(): gathered = lax.all_gather(quarter, 'sect', axis=1, tiled=True)]
    ppermute x8 -> x4, waiting for transfers between devices: 62.2 us -> 52.9 us  [from_behind(): lax.ppermute(array, axis, [(i, (i + by) % size) for i in range(size)])]
    unnamed x28 -> x16, local copies, waits for them, and re-layouts: 28.5 us -> 23.3 us
  transfers between devices with their start and end apart: 16 -> 8, of which waited for: 10 -> 7; matrix products, arithmetic and copies ran while one was open for 11% -> 14% of each run, Pallas kernels for 43% -> 29%
where the time goes in v1:
time: 271 us; the launch traced here: 268 us
  waiting for transfers between devices  125 us (46%)
  Pallas kernels  76.3 us (28%)
  local copies, waits for them, and re-layouts  50.5 us (19%)
  between operations  13.8 us (5%)
    pallas_call x4, Pallas kernels, block_layer(): pl.pallas_call(functools.partial(product_kernel, fanin), grid_spec=pltpu....  76.3 us
    all_gather x4, waiting for transfers between devices, layer(): gathered = lax.all_gather(quarter, 'sect', axis=1, tiled=True)  71.3 us
    ppermute x4, waiting for transfers between devices, from_behind(): lax.ppermute(array, axis, [(i, (i + by) % size) for i in range(size)])  52.9 us
    another operation x1, local copies, waits for them, and re-layouts, per_device(): weights = block_tiles[0].reshape(nblk, fanin * BLK, BLK)  24 us
    unnamed x16, local copies, waits for them, and re-layouts  23.3 us
  transfers between devices with their start and end apart: 8, of which 7 were waited for; matrix products, arithmetic and copies ran while one was open for 14% of the time, Pallas kernels for 29%

profile of v1, /device:TPU:6, one launch (start us, length us, event | category | flops | bytes accessed | tf_op | source)
XLA Modules:
  0.0 267.5 jit_solution(4291498784307365016)
XLA Ops:
  6.5 0.0 all-gather.5.cloned.1.call-start
  6.5 3.1 %fusion = (bf16[64,8192]{1,0:T(8,128)(2,1)}, bf16[64,8192]{1,0:T(8,128)(2,1)}) fusion(bf16[128,8192]{1,0:T(8,128)(2,1)} %param.4), kind=kLoop, calls=%fused_computation.1 | loop fusion | bytes 4194304 | tf_op jit(solution)/shard_map/slice | solution.py:83
  9.6 0.0 all-gather.5.cloned.1.call-update
  9.6 0.0 all-gather.9.cloned.1.call-start
  9.7 0.7 all-gather.9.cloned.1.call-update
  10.4 0.0 all-gather.7.cloned.1.call-start
  10.4 12.5 %copy.6 = bf16[1,128,8,4096]{1,3,2,0:T(8,128)(2,1)} copy(bf16[1,128,8,4096]{3,2,1,0:T(8,128)(2,1)} %param.5) | data formatting | bytes 16777216 | tf_op args[1]
  22.9 0.0 copy-start.6
  22.9 24.0 %copy.7.w_ref = bf16[128,512,64]{2,1,0:T(8,128)(2,1)} copy(bf16[128,512,64]{0,2,1:T(8,128)(2,1)} %bitcast.1) | data formatting | bytes 16777216 | tf_op jit(solution)/shard_map/reshape;squeeze | solution.py:78
  46.9 0.0 copy-done.6
  46.9 0.1 copy.5
  47.0 0.1 reshape_squeeze.6.src_ref
  47.7 14.0 %all-gather.5.cloned.1.call-done.x_ref = bf16[64,32768]{1,0:T(8,128)(2,1)} async-done(((bf16[64,8192]{1,0:T(8,128)(2,1)}), bf16[64,32768]{1,0:T(8,128)(2,1)}) %all-gather.5.cloned.1.call-update) | async-done | bytes 4194320 | tf_op jit(solution)/shard_map/all_gather | solution.py:72
  61.7 0.0 copy-start.2
  61.7 2.2 copy-done.2
  63.9 19.1 %shard_map.46 = bf16[64,8192]{1,0:T(8,128)(2,1)S(1)} custom-call(s32[1024]{0:T(1024)S(1)} %reshape_squeeze.6.src_ref, bf16[64,32768]{1,0:T(8,128)(2,1)S(1)} %copy-done.2, bf16[128,512,64]{2,1,0:T(8,128)(2,1)} %copy.7.w_ref, f32[1]{0:T(128)S(6)} %copy.11.b_ref), custom_call_target="tpu_custom_call" | custom-call | flops 8589934592 | bytes 13631488 | tf_op jit(solution)/shard_map/pallas_call | solution.py:49
  83.0 0.1 collective-permute-start
  83.1 17.6 %collective-permute-done = bf16[64,8192]{1,0:T(8,128)(2,1)S(1)} collective-permute-done((bf16[64,8192]{1,0:T(8,128)(2,1)S(1)}, bf16[64,8192]{1,0:T(8,128)(2,1)S(1)}, u32[]{:S(2)}, u32[]{:S(2)}) %collective-permute-start) | collective-permute-done | bytes 1048608 | tf_op jit(solution)/shard_map/ppermute | solution.py:17
  100.8 0.0 copy-start.4
  100.8 1.0 copy-done.4
  101.8 0.0 all-gather.7.cloned.1.call-update
  101.8 0.0 all-gather.11.cloned.1.call-start
  101.9 12.9 %all-gather.9.cloned.1.call-done.x_ref = bf16[64,32768]{1,0:T(8,128)(2,1)} async-done(((bf16[64,8192]{1,0:T(8,128)(2,1)}), bf16[64,32768]{1,0:T(8,128)(2,1)}) %all-gather.9.cloned.1.call-update) | async-done | bytes 4194320 | tf_op jit(solution)/shard_map/all_gather | solution.py:72
  114.7 0.0 copy-start
  114.7 2.2 copy-done
  116.9 19.1 %shard_map.48 = bf16[64,8192]{1,0:T(8,128)(2,1)S(1)} custom-call(s32[1024]{0:T(1024)S(1)} %reshape_squeeze.6.src_ref, bf16[64,32768]{1,0:T(8,128)(2,1)S(1)} %copy-done, bf16[128,512,64]{2,1,0:T(8,128)(2,1)} %copy.7.w_ref, f32[1]{0:T(128)S(6)} %copy.11.b_ref), custom_call_target="tpu_custom_call" | custom-call | flops 8589934592 | bytes 13631488 | tf_op jit(solution)/shard_map/pallas_call | solution.py:49
  136.1 0.1 collective-permute-start.2
  136.1 17.6 %collective-permute-done.2 = bf16[64,8192]{1,0:T(8,128)(2,1)S(1)} collective-permute-done((bf16[64,8192]{1,0:T(8,128)(2,1)S(1)}, bf16[64,8192]{1,0:T(8,128)(2,1)S(1)}, u32[]{:S(2)}, u32[]{:S(2)}) %collective-permute-start.2) | collective-permute-done | bytes 1048608 | tf_op jit(solution)/shard_map/ppermute | solution.py:17
  153.8 0.0 copy-start.5
  153.8 1.0 copy-done.5
  154.8 0.0 all-gather.11.cloned.1.call-update
  154.8 13.0 %all-gather.7.cloned.1.call-done.x_ref = bf16[64,32768]{1,0:T(8,128)(2,1)} async-done(((bf16[64,8192]{1,0:T(8,128)(2,1)}), bf16[64,32768]{1,0:T(8,128)(2,1)}) %all-gather.7.cloned.1.call-update) | async-done | bytes 4194320 | tf_op jit(solution)/shard_map/all_gather | solution.py:72
  167.7 0.0 copy-start.1
  167.8 2.2 copy-done.1
  169.9 19.1 %shard_map.47 = bf16[64,8192]{1,0:T(8,128)(2,1)S(1)} custom-call(s32[1024]{0:T(1024)S(1)} %reshape_squeeze.6.src_ref, bf16[64,32768]{1,0:T(8,128)(2,1)S(1)} %copy-done.1, bf16[128,512,64]{2,1,0:T(8,128)(2,1)} %copy.7.w_ref, f32[1]{0:T(128)S(6)} %copy.11.b_ref), custom_call_target="tpu_custom_call" | custom-call | flops 8589934592 | bytes 13631488 | tf_op jit(solution)/shard_map/pallas_call | solution.py:49
  189.1 0.1 collective-permute-start.1
  189.2 31.5 %all-gather.11.cloned.1.call-done.x_ref = bf16[64,32768]{1,0:T(8,128)(2,1)} async-done(((bf16[64,8192]{1,0:T(8,128)(2,1)}), bf16[64,32768]{1,0:T(8,128)(2,1)}) %all-gather.11.cloned.1.call-update) | async-done | bytes 4194320 | tf_op jit(solution)/shard_map/all_gather | solution.py:72
  220.6 0.0 copy-start.3
  220.6 2.2 copy-done.3
  222.8 18.9 %shard_map.49 = bf16[64,8192]{1,0:T(8,128)(2,1)S(1)} custom-call(s32[1024]{0:T(1024)S(1)} %reshape_squeeze.6.src_ref, bf16[64,32768]{1,0:T(8,128)(2,1)S(1)} %copy-done.3, bf16[128,512,64]{2,1,0:T(8,128)(2,1)} %copy.7.w_ref, f32[1]{0:T(128)S(6)} %copy.11.b_ref), custom_call_target="tpu_custom_call" | custom-call | flops 8589934592 | bytes 13631488 | tf_op jit(solution)/shard_map/pallas_call | solution.py:49
  241.7 0.1 collective-permute-start.3
  241.8 0.0 collective-permute-done.1
  241.8 17.6 %collective-permute-done.3 = bf16[64,8192]{1,0:T(8,128)(2,1)S(1)} collective-permute-done((bf16[64,8192]{1,0:T(8,128)(2,1)S(1)}, bf16[64,8192]{1,0:T(8,128)(2,1)S(1)}, u32[]{:S(2)}, u32[]{:S(2)}) %collective-permute-start.3) | collective-permute-done | bytes 1048608 | tf_op jit(solution)/shard_map/ppermute | solution.py:17
  259.5 1.5 pad_maximum_fusion
Async XLA Ops:
  6.5 55.2 %all-gather.5.cloned.1.call-start = ((), (), s32[]{:S(2)}) async-start(), calls=%async_computation | async-start | bytes 5242880 | tf_op jit(solution)/shard_map/all_gather | solution.py:72
  9.6 105.1 %all-gather.9.cloned.1.call-start = ((), (), s32[]{:S(2)}) async-start(), calls=%async_computation.2 | async-start | bytes 5242880 | tf_op jit(solution)/shard_map/all_gather | solution.py:72
  10.4 157.4 %all-gather.7.cloned.1.call-start = ((), (), s32[]{:S(2)}) async-start(), calls=%async_computation.1 | async-start | bytes 5242880 | tf_op jit(solution)/shard_map/all_gather | solution.py:72
  22.9 24.0 %copy-start.6 = (s32[1,128,8]{1,2,0:T(8,128)S(1)}, s32[1,128,8]{1,2,0:T(8,128)}, u32[]{:S(2)}) copy-start(s32[1,128,8]{1,2,0:T(8,128)} %param.6) | copy-start | bytes 12292
  61.7 2.2 copy-start.2
  83.0 17.7 %collective-permute-start = (bf16[64,8192]{1,0:T(8,128)(2,1)S(1)}, bf16[64,8192]{1,0:T(8,128)(2,1)S(1)}, u32[]{:S(2)}, u32[]{:S(2)}) collective-permute-start(bf16[64,8192]{1,0:T(8,128)(2,1)S(1)} %shard_map.46), channel_id=1, source_target_pairs={{0,4},{4,8},{8,12},{12,16},{16,20},{20,24},{24,28},{28,32},{32,36}... | collective-permute-start | bytes 3145736 | tf_op jit(solution)/shard_map/ppermute | solution.py:17
  100.8 1.0 copy-start.4
  101.8 118.8 %all-gather.11.cloned.1.call-start = ((), (), s32[]{:S(2)}) async-start(), calls=%async_computation.3 | async-start | bytes 5242880 | tf_op jit(solution)/shard_map/all_gather | solution.py:72
  114.7 2.2 copy-start
  136.1 17.7 %collective-permute-start.2 = (bf16[64,8192]{1,0:T(8,128)(2,1)S(1)}, bf16[64,8192]{1,0:T(8,128)(2,1)S(1)}, u32[]{:S(2)}, u32[]{:S(2)}) collective-permute-start(bf16[64,8192]{1,0:T(8,128)(2,1)S(1)} %shard_map.48), channel_id=1, source_target_pairs={{0,4},{4,8},{8,12},{12,16},{16,20},{20,24},{24,28},{28,32},{32,36}... | collective-permute-start | bytes 3145736 | tf_op jit(solution)/shard_map/ppermute | solution.py:17
  153.8 1.0 copy-start.5
  167.7 2.2 copy-start.1
  189.1 52.8 %collective-permute-start.1 = (bf16[64,8192]{1,0:T(8,128)(2,1)S(1)}, bf16[64,8192]{1,0:T(8,128)(2,1)S(1)}, u32[]{:S(2)}, u32[]{:S(2)}) collective-permute-start(bf16[64,8192]{1,0:T(8,128)(2,1)S(1)} %shard_map.47), channel_id=1, source_target_pairs={{0,4},{4,8},{8,12},{12,16},{16,20},{20,24},{24,28},{28,32},{32,36}... | collective-permute-start | bytes 3145736 | tf_op jit(solution)/shard_map/ppermute | solution.py:17
  220.6 2.2 copy-start.3
  241.7 17.7 %collective-permute-start.3 = (bf16[64,8192]{1,0:T(8,128)(2,1)S(1)}, bf16[64,8192]{1,0:T(8,128)(2,1)S(1)}, u32[]{:S(2)}, u32[]{:S(2)}) collective-permute-start(bf16[64,8192]{1,0:T(8,128)(2,1)S(1)} %shard_map.49), channel_id=1, source_target_pairs={{0,4},{4,8},{8,12},{12,16},{16,20},{20,24},{24,28},{28,32},{32,36}... | collective-permute-start | bytes 3145736 | tf_op jit(solution)/shard_map/ppermute | solution.py:17
Sparse Core Ops, SparseCore 0:
  9.8 51.9 all-gather.4
  63.5 51.1 all-gather.8
  116.5 51.1 all-gather.6
  169.4 51.1 all-gather.10
